TPU v7x, 128 devices: a whole 4x4x4 slice. The times are simulated.
128 devices in a mesh: pop: 8 (over y_lo, x), col: 16 (over z, y_hi, core).
Axes of the slice: x: 4, y: 4 (y_hi: 2, y_lo: 2; y = y_hi * 2 + y_lo), z: 4, core: 2. Of those that a mesh axis runs over, the one named last changes fastest.
Arguments:
- acts: bfloat16 [128, 64, 3584], P('pop', None, 'col'), may hold values from -6 to 6
- weight: bfloat16 [3584, 18944], P('pop', 'col'), may hold values from -0.09375 to 0.09375
- input_noise_factor: bfloat16 [128, 4, 3584], P('pop'), may hold values from -1 to 1
- output_noise_factor: bfloat16 [128, 4, 18944], P('pop', None, 'col'), may hold values from -8 to 8
- ranks: int32 [128], P('pop'), may hold values from 0 to 127, each once
Outputs:
- member_out: bfloat16 [128, 64, 18944], P('pop', None, 'col')
- step_dir: float32 [3584, 18944], P('pop', 'col')
- new_weight: bfloat16 [3584, 18944], P('pop', 'col')
Inputs may be any that keep to these rules, and one draw needn't show every extreme that they name: `ranks`: every member has a different rank.
All inputs are finite; a program needn't handle non-finite values.
Results may differ from a plain program's by a relative error of at most 0.0034.
Values may be sent and summed in bfloat16 or wider, within the bound.
A program may use at most 192 MiB of HBM per device.

v0:
```python
import jax
import jax.numpy as jnp
from jax import lax
from jax.sharding import PartitionSpec as P

D = 3584
F = 18944


def body(acts, weight, input_noise_factor, output_noise_factor, ranks):
    whole = lax.all_gather(acts, "col", axis=2, tiled=True)
    members, tokens, width = whole.shape
    flat = whole.reshape(members * tokens, width)
    base = jnp.dot(
        flat, lax.all_gather(weight, "pop", axis=0, tiled=True), preferred_element_type=jnp.float32
    )
    lower_bound = jnp.einsum(
        "mtd,mrd->mtr", whole, input_noise_factor, preferred_element_type=jnp.float32
    )
    pert = jnp.einsum(
        "zlh,zhj->zlj",
        lower_bound,
        output_noise_factor.astype(jnp.float32),
        precision=lax.Precision.HIGHEST,
    )
    member_out = (base.reshape(members, tokens, -1) + 0.5 * pert).astype(jnp.bfloat16)
    pop_count = lax.axis_size("pop")
    total_members = ranks.shape[0] * pop_count
    fit = ranks.astype(jnp.float32) / (total_members - 1) - 0.5
    scaled_update = (output_noise_factor.astype(jnp.float32) * fit[:, None, None]).astype(
        jnp.bfloat16
    )
    weight_change = lax.psum_scatter(
        jnp.einsum(
            "vjs,vjg->sg", input_noise_factor, scaled_update, preferred_element_type=jnp.float32
        ),
        "pop",
        scatter_dimension=0,
        tiled=True,
    )
    mean_sq = lax.psum(jnp.sum(weight_change * weight_change), ("pop", "col")) / (D * F)
    step_dir = weight_change * lax.rsqrt(mean_sq + 1e-06)
    new_weight = (weight.astype(jnp.float32) + 0.01 * step_dir).astype(jnp.bfloat16)
    return (member_out, step_dir, new_weight)


def solution(mesh):
    in_specs = (
        P("pop", None, "col"),
        P("pop", "col"),
        P("pop", None, None),
        P("pop", None, "col"),
        P("pop"),
    )
    out_specs = (P("pop", None, "col"), P("pop", "col"), P("pop", "col"))
    return jax.shard_map(body, mesh=mesh, in_specs=in_specs, out_specs=out_specs, check_vma=False)
```

profile of v0, /device:TPU:1, one launch (start us, length us, event | category | flops | bytes accessed | tf_op | source)
XLA Modules:
  0.0 489.5 jit_solution(12580459237026647606)
XLA Ops:
  7.2 0.0 copy-start
  7.2 0.0 all-gather.3.cloned.1.call-start
  7.2 2.7 copy.13
  10.0 0.0 all-gather.3.cloned.1.call-update
  10.0 0.0 all-gather.5.cloned.1.call-start
  10.0 0.7 all-gather.5.cloned.1.call-update
  10.7 0.0 reduce-scatter.4.cloned.1.call-start
  10.8 0.7 multiply_add_fusion
  11.4 1.0 multiply_convert_fusion
  12.5 0.0 copy-done
  12.5 8.2 %convolution_bitcast_fusion = f32[3584,1184]{0,1:T(8,128)} fusion(bf16[16,4,3584]{2,1,0:T(4,128)(2,1)S(1)} %copy-done, bf16[16,4,1184]{2,1,0:T(4,128)(2,1)S(1)} %multiply_convert_fusion), kind=kOutput, calls=%fused_computation | convolution fusion | flops 543162368 | bytes 17584128 | tf_op jit(solution)/shard_map/vjs,vjg->sg/dot_general | solution.py:34
  20.7 19.0 %copy.20 = f32[3584,1184]{1,0:T(8,128)} copy(f32[3584,1184]{0,1:T(8,128)} %convolution_bitcast_fusion) | data formatting | bytes 33947648
  39.7 0.0 copy-start.3
  39.7 0.0 reduce-scatter.4.cloned.1.call-update
  39.7 1.2 copy-done.3
  41.0 1.5 copy.17
  42.5 71.7 %all-gather.3.cloned.1.call-done = bf16[16,64,3584]{1,0,2:T(8,128)(2,1)} async-done(((bf16[16,64,224]{1,0,2:T(8,128)(2,1)}), bf16[16,64,3584]{1,0,2:T(8,128)(2,1)}) %all-gather.3.cloned.1.call-update) | async-done | bytes 7340048 | tf_op jit(solution)/shard_map/all_gather | solution.py:11
  114.2 16.3 %copy.14 = bf16[16,64,3584]{2,1,0:T(8,128)(2,1)} copy(bf16[16,64,3584]{1,0,2:T(8,128)(2,1)} %all-gather.3.cloned.1.call-done) | data formatting | bytes 14680064 | tf_op jit(solution)/shard_map/all_gather | solution.py:11
  130.4 5.1 %fusion.4 = f32[16,64,4]{1,2,0:T(4,128)S(1)} fusion(bf16[16,64,3584]{2,1,0:T(8,128)(2,1)} %copy.14, bf16[16,4,3584]{2,1,0:T(4,128)(2,1)S(1)} %copy-done), kind=kOutput, calls=%fused_computation.11 | convolution fusion | flops 29360128 | bytes 7815168 | tf_op jit(solution)/shard_map/mtd,mrd->mtr/dot_general | solution.py:17
  135.5 76.5 %all-gather.5.cloned.1.call-done = bf16[3584,1184]{1,0:T(8,128)(2,1)} async-done(((bf16[448,1184]{1,0:T(8,128)(2,1)}), bf16[3584,1184]{1,0:T(8,128)(2,1)}) %all-gather.5.cloned.1.call-update) | async-done | bytes 8486928 | tf_op jit(solution)/shard_map/all_gather | solution.py:15
  212.0 16.1 %fusion = f32[16,64,1184]{2,1,0:T(8,128)} fusion(bf16[16,64,3584]{2,1,0:T(8,128)(2,1)} %copy.14, bf16[3584,1184]{1,0:T(8,128)(2,1)} %all-gather.5.cloned.1.call-done), kind=kOutput, calls=%fused_computation.1 | convolution fusion | flops 8690597888 | bytes 20676608 | tf_op jit(solution)/shard_map/dot_general | solution.py:14
  228.1 0.0 copy-start.4
  228.1 171.4 %reduce-scatter.4.cloned.1.call-done = f32[448,1184]{1,0:T(8,128)} async-done(((f32[3584,1184]{1,0:T(8,128)}), f32[448,1184]{1,0:T(8,128)}) %reduce-scatter.4.cloned.1.call-update) | async-done | bytes 2121744
  399.5 2.3 copy.21
  401.8 1.2 multiply_reduce_fusion
  403.0 0.0 copy-done.4
  403.1 6.3 %add_convert_fusion = bf16[16,64,1184]{2,1,0:T(8,128)(2,1)} fusion(f32[16,64,1184]{2,1,0:T(8,128)} %fusion, f32[16,64,4]{1,2,0:T(4,128)S(1)} %fusion.4, bf16[16,4,1184]{2,1,0:T(4,128)(2,1)S(1)} %copy-done.4), kind=kOutput, calls=%fused_computation.3 | convolution fusion | flops 61833216 | bytes 7442432 | tf_op jit(solution)/shard_map/zlh,zhj->zlj/dot_general | solution.py:20
  409.4 64.5 %psum.7 = f32[]{:T(128)} all-reduce(f32[]{:T(128)} %multiply_reduce_fusion), channel_id=1, replica_groups=mesh['pop'=8,'col'=16] {'pop','col'}, use_global_device_ids=true, to_apply=%region_2.0 | all-reduce | flops 1 | bytes 8 | tf_op jit(solution)/shard_map/psum | solution.py:41
  474.6 0.0 copy-start.1
  474.6 3.6 add_convert_fusion.1
  478.2 0.0 copy-start.2
  478.2 3.2 copy.18
  481.4 0.0 copy-done.2
  481.4 1.5 copy.19
  483.0 0.0 copy-done.1
Async XLA Ops:
  7.2 5.3 %copy-start = (bf16[16,4,3584]{2,1,0:T(4,128)(2,1)S(1)}, bf16[16,4,3584]{2,1,0:T(4,128)(2,1)}, u32[]{:S(2)}) copy-start(bf16[16,4,3584]{2,1,0:T(4,128)(2,1)} %param.7) | copy-start | bytes 1376260
  7.2 107.0 %all-gather.3.cloned.1.call-start = ((), (), s32[]{:S(2)}) async-start(), calls=%async_computation.1 | async-start | bytes 15597568 | tf_op jit(solution)/shard_map/all_gather | solution.py:11
  10.0 202.0 %all-gather.5.cloned.1.call-start = ((), (), s32[]{:S(2)}) async-start(), calls=%async_computation.2 | async-start | bytes 10321920 | tf_op jit(solution)/shard_map/all_gather | solution.py:15
  10.7 388.8 %reduce-scatter.4.cloned.1.call-start = ((), (), s32[]{:S(2)}) async-start(), calls=%async_computation.3 | async-start | bytes 20643840
  39.7 1.3 copy-start.3
  228.1 175.0 %copy-start.4 = (bf16[16,4,1184]{2,1,0:T(4,128)(2,1)S(1)}, bf16[16,4,1184]{2,1,0:T(4,128)(2,1)}, u32[]{:S(2)}) copy-start(bf16[16,4,1184]{2,1,0:T(4,128)(2,1)} %param.8) | copy-start | bytes 454660
  474.6 8.4 %copy-start.1 = (bf16[16,4,3584]{2,1,0:T(4,128)(2,1)S(1)}, bf16[16,4,3584]{2,1,0:T(4,128)(2,1)}, u32[]{:S(2)}) copy-start(bf16[16,4,3584]{2,1,0:T(4,128)(2,1)} %param.7) | copy-start | bytes 1376260
  478.2 3.2 copy-start.2
Sparse Core Ops, SparseCore 0:
  11.0 103.0 all-gather.2
  115.8 96.1 all-gather.4
  214.5 184.9 reduce-scatter.3
where the time goes:
time: 491 us; the launch traced here: 489 us
  waiting for transfers between devices  320 us (65%)
  blocking collectives  64.5 us (13%)
  local copies, waits for them, and re-layouts  47.8 us (10%)
  matrix products  35.7 us (7%)
  between operations  14.5 us (3%)
  other arithmetic  6.53 us (1%)
    unnamed x4, waiting for transfers between devices  172 us
    all_gather x1, waiting for transfers between devices, body(): lax.all_gather(weight, 'pop', axis=0, tiled=True)  76.5 us
    all_gather x1, waiting for transfers between devices, body(): whole = lax.all_gather(acts, 'col', axis=2, tiled=True)  71.7 us
    psum x1, blocking collectives, body(): lax.psum(jnp.sum(weight_change * weight_change), ('pop', 'col')) / (D * F)  64.5 us
    unnamed x16, local copies, waits for them, and re-layouts  31.5 us
    all_gather x1, local copies, waits for them, and re-layouts, body(): whole = lax.all_gather(acts, 'col', axis=2, tiled=True)  16.3 us
    dot_general x1, matrix products, body(): jnp.dot(flat, lax.all_gather(weight, 'pop', axis=0, tiled=True), preferre...  16.1 us
  transfers between devices with their start and end apart: 3, of which 3 were waited for; matrix products, arithmetic and copies ran while one was open for 14% of the time, Pallas kernels for 0%

commit v1 on v0

v1 whole, which is shorter than its diff:
```python
import functools

import jax
import jax.numpy as jnp
from jax import lax
from jax.experimental import pallas as pl
from jax.experimental.pallas import tpu as pltpu
from jax.sharding import PartitionSpec as P

D = 3584
F = 18944
NX = 4
NZ = 4
POP = 8
COL = 16
ROWS = 448
WIDE = 1184
FEAT = 224
TOKENS = 1024
PART = 64
CHUNK = 112
TILE = 256
MESH = pl.DeviceIdType.MESH
BF16 = jnp.bfloat16
F32 = jnp.float32


def kernel(
    acts,
    weight,
    noise,
    scaled,
    out_noise,
    out,
    delta_out,
    total_out,
    wbuf,
    xbuf,
    abuf,
    bbuf,
    acc,
    low,
    delta,
    obuf,
    part,
    parts,
    wsem,
    bsem,
    asem,
    xsem,
    rsem,
    ssem,
    lsem,
):
    pop, col = lax.axis_index("pop"), lax.axis_index("col")
    x, ylo = pop % NX, pop // NX
    z, yhi, core = col // 4, (col // 2) % 2, col % 2

    def pop_at(dy, dx):
        return (ylo * (1 - 2 * dy) + dy) * NX + (x + dx) % NX

    def col_at(dz, dy, dc):
        return (
            ((z + dz) % NZ) * 4
            + (yhi * (1 - 2 * dy) + dy) * 2
            + (core * (1 - 2 * dc) + dc)
        )

    right, left = (pop_at(0, 1), col), (pop_at(0, 3), col)
    pair = (pop_at(1, 0), col)
    up, down = (pop, col_at(1, 0, 0)), (pop, col_at(3, 0, 0))
    far, twin = (pop, col_at(0, 1, 0)), (pop, col_at(0, 0, 1))
    opposite = (pop, col_at(2, 0, 0))
    pop_peers = [
        (dy, dx, (pop_at(dy, dx), col))
        for dy in range(2)
        for dx in range(NX)
        if dy + dx > 0
    ]

    sent = []

    def send(src, dst, sem, device):
        copy = pltpu.make_async_remote_copy(
            src_ref=src,
            dst_ref=dst,
            send_sem=ssem.at[len(sent)],
            recv_sem=sem,
            device_id=device,
            device_id_type=MESH,
        )
        copy.start()
        sent.append(copy)

    def arrive(dst, sem):
        pltpu.make_async_remote_copy(
            src_ref=dst,
            dst_ref=dst,
            send_sem=ssem.at[0],
            recv_sem=sem,
            device_id=right,
            device_id_type=MESH,
        ).wait_recv()

    own = [
        pltpu.make_async_copy(weight, wbuf.at[0], lsem.at[0]),
        pltpu.make_async_copy(acts, xbuf.at[col], lsem.at[1]),
        pltpu.make_async_copy(
            noise.at[pl.ds(2 * pop, 2)], abuf.at[:, pl.ds(0, PART), :], lsem.at[2]
        ),
        pltpu.make_async_copy(scaled, bbuf.at[pl.ds(0, PART), :], lsem.at[3]),
    ]
    for copy in own:
        copy.start()

    barrier = pltpu.get_barrier_semaphore()
    peers = [device for _, _, device in pop_peers] + [up, down, opposite, far, twin]
    for device in peers:
        pl.semaphore_signal(barrier, inc=1, device_id=device, device_id_type=MESH)
    pl.semaphore_wait(barrier, len(peers))

    def w_at(slot, k):
        return wbuf.at[slot, pl.ds(k * CHUNK, CHUNK), :]

    def b_at(slot, k):
        return bbuf.at[pl.ds(slot * PART + k * 32, 32), :]

    def w_send(src_slot, k, dst_slot, device):
        src = weight.at[pl.ds(k * CHUNK, CHUNK), :] if src_slot == 0 else w_at(src_slot, k)
        send(src, w_at(dst_slot, k), wsem.at[dst_slot * 4 + k], device)

    def b_send(src_slot, k, dst_slot, device):
        src = scaled.at[pl.ds(k * 32, 32), :] if src_slot == 0 else b_at(src_slot, k)
        send(src, b_at(dst_slot, k), bsem.at[dst_slot * 2 + k], device)

    def w_arrive(slot, k):
        arrive(w_at(slot, k), wsem.at[slot * 4 + k])

    def b_arrive(slot, k):
        arrive(b_at(slot, k), bsem.at[slot * 2 + k])

    def x_at(c, half=None):
        if half is None:
            return xbuf.at[c]
        return xbuf.at[c, pl.ds(half * (TOKENS // 2), TOKENS // 2), :]

    def x_send(c, half, sem, device, src=None):
        send(x_at(c, half) if src is None else src, x_at(c, half), xsem.at[sem], device)

    for k, device, slot in ((0, right, 3), (1, left, 1), (0, pair, 4), (1, right, 3), (0, left, 1), (1, pair, 4)):
        b_send(0, k, slot, device)
    x_send(col, None, 0, up, acts)
    x_send(col, None, 1, down, acts)
    x_send(col, None, 2, far, acts)
    x_send(col, None, 9, twin, acts)
    for dy, dx, device in pop_peers:
        slot = dy * NX + (NX - dx) % NX
        send(
            noise.at[pl.ds(2 * device[0], 2)],
            abuf.at[:, pl.ds(slot * PART, PART), :],
            asem.at[slot],
            device,
        )
    for k in range(2):
        w_send(0, k, 3, right)
        w_send(0, 3 - k, 1, left)
        w_send(0, k, 4, pair)

    b_arrive(3, 0)
    b_send(3, 0, 2, right)
    b_arrive(1, 1)
    b_send(1, 1, 2, left)
    for k in range(2):
        b_arrive(4, k)
        b_send(4, k, 7, right)
        b_send(4, k, 5, left)
    for k in range(2):
        w_send(0, 2 + k, 3, right)
        w_send(0, 1 - k, 1, left)
        w_send(0, 2 + k, 4, pair)

    c_down, c_up = col_at(3, 0, 0), col_at(1, 0, 0)
    c_far, c_opp = col_at(0, 1, 0), col_at(2, 0, 0)
    f_down, f_up, f_opp = col_at(3, 1, 0), col_at(1, 1, 0), col_at(2, 1, 0)

    def add_low(c):
        low[...] += lax.dot_general(
            xbuf[c],
            noise[c],
            (((1,), (1,)), ((), ())),
            preferred_element_type=F32,
        )

    def x_arrive(c, half, sem):
        arrive(x_at(c, half), xsem.at[sem])

    x_arrive(c_down, None, 0)
    x_send(c_down, 0, 5, up)
    x_send(c_down, None, 10, twin)
    x_arrive(c_up, None, 1)
    x_send(c_up, 1, 6, down)
    x_send(c_up, None, 11, twin)
    x_arrive(c_far, None, 2)
    x_send(c_far, None, 3, up)
    x_send(c_far, None, 4, down)
    x_send(c_far, None, 12, twin)
    for k in range(2):
        b_arrive(2, k)
        b_send(2, k, 6, pair)

    for copy in own:
        copy.wait()
    low[...] = jnp.zeros_like(low)
    for c in (col, c_down, c_up, c_far):
        add_low(c)

    w_arrive(3, 0)
    w_send(3, 0, 2, right)
    w_arrive(1, 3)
    w_send(1, 3, 2, left)
    w_arrive(3, 1)
    w_send(3, 1, 2, right)
    w_arrive(1, 2)
    w_send(1, 2, 2, left)

    b_arrive(3, 1)
    b_arrive(1, 0)
    for slot in (7, 5, 6):
        for k in range(2):
            b_arrive(slot, k)
    for slot in range(1, POP):
        arrive(abuf.at[:, pl.ds(slot * PART, PART), :], asem.at[slot])
    squares = jnp.zeros((), F32)
    for h in range(2):
        block = lax.dot_general(
            abuf[h], bbuf[...], (((0,), (0,)), ((), ())), preferred_element_type=F32
        )
        delta[pl.ds(h * FEAT, FEAT), :] = block
        squares += jnp.sum(block * block)
    write_delta = pltpu.make_async_copy(delta, delta_out, lsem.at[4])
    write_delta.start()
    part[0] = jnp.full((8, 128), squares, F32)

    for k in range(4):
        w_arrive(4, k)
    x_arrive(f_down, None, 3)
    x_send(f_down, 0, 7, up)
    x_send(f_down, None, 13, twin)
    x_arrive(f_up, None, 4)
    x_send(f_up, 1, 8, down)
    x_send(f_up, None, 14, twin)

    send(part.at[0], parts.at[0], rsem.at[0], twin)
    arrive(parts.at[0], rsem.at[0])
    part[1] = part[0] + parts[0]
    add_low(f_down)
    add_low(f_up)
    for i, device in enumerate((up, opposite, down)):
        send(part.at[1], parts.at[1 + i], rsem.at[1 + i], device)
    for i in range(3):
        arrive(parts.at[1 + i], rsem.at[1 + i])
    part[2] = part[1] + parts[1] + parts[2] + parts[3]

    x_arrive(c_opp, 0, 5)
    x_send(c_opp, 0, 15, twin)
    x_arrive(c_opp, 1, 6)
    x_send(c_opp, 1, 16, twin)
    add_low(c_opp)
    send(part.at[2], parts.at[4], rsem.at[4], far)
    arrive(parts.at[4], rsem.at[4])
    part[3] = part[2] + parts[4]
    for k in range(2):
        w_send(4, k, 7, right)
        w_send(4, k, 5, left)
    x_arrive(f_opp, 0, 7)
    x_send(f_opp, 0, 17, twin)
    x_arrive(f_opp, 1, 8)
    x_send(f_opp, 1, 18, twin)
    add_low(f_opp)
    for dy, dx, device in pop_peers:
        i = 4 + dy * NX + dx
        send(part.at[3], parts.at[i], rsem.at[i], device)
    for k in range(2, 4):
        w_send(4, k, 7, right)
        w_send(4, k, 5, left)

    for k in (0, 3):
        w_arrive(2, k)
        w_send(2, k, 6, pair)
    for (dz, dy), sems in (
        ((0, 0), ((None, 9),)),
        ((3, 0), ((None, 10),)),
        ((1, 0), ((None, 11),)),
        ((0, 1), ((None, 12),)),
        ((3, 1), ((None, 13),)),
        ((1, 1), ((None, 14),)),
        ((2, 0), ((0, 15), (1, 16))),
        ((2, 1), ((0, 17), (1, 18))),
    ):
        c = col_at(dz, dy, 1)
        for half, sem in sems:
            x_arrive(c, half, sem)
        add_low(c)
    for k in (1, 2):
        w_arrive(2, k)
        w_send(2, k, 6, pair)

    rank = lax.broadcasted_iota(jnp.int32, (TOKENS, PART), 1) // 4
    token = lax.broadcasted_iota(jnp.int32, (TOKENS, PART), 0) // 64
    rest = jnp.where(rank == token, low[...] * 0.5, 0.0)
    low[...] = rest

    def rows(i):
        return pl.ds(pl.multiple_of(i * TILE, TILE), TILE)

    @pl.loop(0, TOKENS // TILE)
    def _(i):
        left_over = low[rows(i), :]
        total = None
        for _ in range(3):
            term = left_over.astype(BF16)
            left_over = left_over - term.astype(F32)
            product = jnp.dot(term, out_noise[...], preferred_element_type=F32)
            total = product if total is None else total + product
        acc[rows(i), :] = total

    def dot(i, slot, h):
        c = 2 * pop_at(slot // NX, slot % NX) + h
        return jnp.dot(
            xbuf[c, rows(i), :],
            wbuf[slot, pl.ds(h * FEAT, FEAT), :],
            preferred_element_type=F32,
        )

    def blocks(slots, halves):
        @pl.loop(0, TOKENS // TILE)
        def _(i):
            for slot in slots:
                for h in halves:
                    acc[rows(i), :] += dot(i, slot, h)

    blocks((0, 4), (0, 1))
    for k in range(2, 4):
        w_arrive(3, k)
    for k in range(2):
        w_arrive(1, k)
    blocks((1, 3), (0, 1))
    blocks((2,), (0, 1))

    total = part[3]
    for dy, dx, device in pop_peers:
        slot = 4 + dy * NX + dx
        arrive(parts.at[slot], rsem.at[slot])
        total = total + parts[slot]
    part[4] = total
    write_total = pltpu.make_async_copy(part.at[4], total_out, lsem.at[5])
    write_total.start()

    for slot in (7, 5):
        for k in range(2):
            w_arrive(slot, k)
    for k in (0, 1):
        w_arrive(6, k)
    blocks((5, 7, 6), (0,))
    for slot in (7, 5):
        for k in range(2, 4):
            w_arrive(slot, k)
    for k in (3, 2):
        w_arrive(6, k)

    for i in range(TOKENS // TILE):
        tile = pl.ds(i * TILE, TILE)
        value = acc[tile, :]
        for slot in (5, 7, 6):
            value = value + dot(i, slot, 1)
        obuf[tile, :] = value.astype(BF16)
        pltpu.make_async_copy(obuf.at[tile, :], out.at[tile, :], lsem.at[6 + i]).start()

    for i in range(TOKENS // TILE):
        tile = pl.ds(i * TILE, TILE)
        pltpu.make_async_copy(obuf.at[tile, :], out.at[tile, :], lsem.at[6 + i]).wait()
    write_delta.wait()
    write_total.wait()
    for copy in sent:
        copy.wait_send()


def body(acts, weight, input_noise_factor, output_noise_factor, ranks):
    fit = ranks.astype(F32) / (16 * POP - 1) - 0.5
    scaled = (output_noise_factor.astype(F32) * fit[:, None, None]).astype(BF16)
    noise = input_noise_factor.reshape(PART, COL, FEAT).transpose(1, 0, 2)
    anywhere = pl.BlockSpec(memory_space=pl.ANY)
    vmem = pl.BlockSpec(memory_space=pltpu.VMEM)
    flat, delta, total = pl.pallas_call(
        kernel,
        out_shape=(
            jax.ShapeDtypeStruct((TOKENS, WIDE), BF16),
            jax.ShapeDtypeStruct((ROWS, WIDE), F32),
            jax.ShapeDtypeStruct((8, 128), F32),
        ),
        in_specs=[anywhere, anywhere, vmem, anywhere, vmem],
        out_specs=(anywhere, anywhere, anywhere),
        scratch_shapes=[
            pltpu.VMEM((POP, ROWS, WIDE), BF16),
            pltpu.VMEM((COL, TOKENS, FEAT), BF16),
            pltpu.VMEM((2, POP * PART, FEAT), BF16),
            pltpu.VMEM((POP * PART, WIDE), BF16),
            pltpu.VMEM((TOKENS, WIDE), F32),
            pltpu.VMEM((TOKENS, PART), F32),
            pltpu.VMEM((ROWS, WIDE), F32),
            pltpu.VMEM((TOKENS, WIDE), BF16),
            pltpu.VMEM((5, 8, 128), F32),
            pltpu.VMEM((12, 8, 128), F32),
            pltpu.SemaphoreType.DMA((POP * 4,)),
            pltpu.SemaphoreType.DMA((POP * 2,)),
            pltpu.SemaphoreType.DMA((POP,)),
            pltpu.SemaphoreType.DMA((19,)),
            pltpu.SemaphoreType.DMA((12,)),
            pltpu.SemaphoreType.DMA((96,)),
            pltpu.SemaphoreType.DMA((10,)),
        ],
        compiler_params=pltpu.CompilerParams(
            collective_id=0, has_side_effects=True, vmem_limit_bytes=62 * 1024 * 1024
        ),
    )(
        acts.reshape(TOKENS, FEAT),
        weight,
        noise,
        scaled.reshape(PART, WIDE),
        output_noise_factor.reshape(PART, WIDE),
    )
    mean_sq = total[0, 0] / (D * F)
    step_dir = delta * lax.rsqrt(mean_sq + 1e-06)
    new_weight = (weight.astype(F32) + 0.01 * step_dir).astype(BF16)
    return (flat.reshape(16, 64, WIDE), step_dir, new_weight)


def solution(mesh):
    in_specs = (
        P("pop", None, "col"),
        P("pop", "col"),
        P("pop", None, None),
        P("pop", None, "col"),
        P("pop"),
    )
    out_specs = (P("pop", None, "col"), P("pop", "col"), P("pop", "col"))
    return jax.shard_map(body, mesh=mesh, in_specs=in_specs, out_specs=out_specs, check_vma=False)
```

time: 491 us -> 116 us (0.24)
  waiting for transfers between devices: 320 us -> 0 us
  Pallas kernels: 0 us -> 98.8 us
  blocking collectives: 64.5 us -> 0 us
  local copies, waits for them, and re-layouts: 47.8 us -> 7.83 us
  matrix products: 35.7 us -> 0 us
  between operations: 14.5 us -> 1.36 us
    unnamed x4 -> x0, waiting for transfers between devices: 172 us -> none
    all_gather x2 -> x0, waiting for transfers between devices: 148 us -> none  [the longest x1 76.5 us: body(): lax.all_gather(weight, 'pop', axis=0, tiled=True)]
    pallas_call x0 -> x1, Pallas kernels: none -> 98.8 us  [body(): pl.pallas_call(kernel, out_shape=(jax.ShapeDtypeStruct((TOKENS, WIDE), BF...]
    psum x1 -> x0, blocking collectives: 64.5 us -> none  [body(): lax.psum(jnp.sum(weight_change * weight_change), ('pop', 'col')) / (D * F)]
    dot_general x4 -> x0, matrix products: 35.7 us -> none  [the longest x1 16.1 us: body(): jnp.dot(flat, lax.all_gather(weight, 'pop', axis=0, tiled=True), preferre...]
    unnamed x16 -> x5, local copies, waits for them, and re-layouts: 31.5 us -> 1.5 us
    all_gather x1 -> x0, local copies, waits for them, and re-layouts: 16.3 us -> none  [body(): whole = lax.all_gather(acts, 'col', axis=2, tiled=True)]
    reshape x0 -> x4, local copies, waits for them, and re-layouts: none -> 5.14 us  [the longest x2 2.79 us: body(): noise = input_noise_factor.reshape(PART, COL, FEAT).transpose(1, 0, 2)]
  transfers between devices with their start and end apart: 3 -> 0, of which waited for: 3 -> 0; matrix products, arithmetic and copies ran while one was open for 14% -> 0% of each run, Pallas kernels for 0% -> 0%
where the time goes in v1:
time: 116 us; the launch traced here: 114 us
  Pallas kernels  98.8 us (85%)
  local copies, waits for them, and re-layouts  7.83 us (7%)
  other arithmetic  5.59 us (5%)
  between operations  1.36 us (1%)
    pallas_call x1, Pallas kernels, body(): pl.pallas_call(kernel, out_shape=(jax.ShapeDtypeStruct((TOKENS, WIDE), BF...  98.8 us
    convert_element_type x1, other arithmetic, body(): new_weight = (weight.astype(F32) + 0.01 * step_dir).astype(BF16)  3.89 us
    reshape x2, local copies, waits for them, and re-layouts, body(): noise = input_noise_factor.reshape(PART, COL, FEAT).transpose(1, 0, 2)  2.79 us

profile of v1, /device:TPU:1, one launch (start us, length us, event | category | flops | bytes accessed | tf_op | source)
XLA Modules:
  0.0 113.6 jit_solution(6718521460719970728)
XLA Ops:
  0.6 0.7 multiply_add_fusion
  1.3 1.0 multiply_convert_fusion
  2.3 0.7 reshape.29.scaled
  3.1 1.6 %reshape.30.out_noise = bf16[64,1184]{1,0:T(8,128)(2,1)} reshape(bf16[16,4,1184]{2,1,0:T(4,128)(2,1)} %param.8) | data formatting | bytes 303104 | tf_op jit(solution)/shard_map/reshape | solution.py:430
  4.7 0.0 copy-start
  4.7 1.8 %reshape.28 = bf16[64,16,224]{2,1,0:T(8,128)(2,1)S(1)} reshape(bf16[16,4,3584]{2,1,0:T(4,128)(2,1)} %param.7) | data formatting | bytes 917504 | tf_op jit(solution)/shard_map/reshape | solution.py:391
  6.5 1.0 copy.10
  7.5 98.8 %shard_map.76 = (bf16[1024,1184]{1,0:T(8,128)(2,1)}, f32[448,1184]{1,0:T(8,128)}, f32[8,128]{1,0:T(8,128)}) custom-call(bf16[1024,224]{1,0:T(8,128)(2,1)} %bitcast.8, bf16[448,1184]{1,0:T(8,128)(2,1)} %weight.1, bf16[16,64,224]{2,1,0:T(8,128)(2,1)} %bitcast.7, bf16[64,1184]{1,0:T(8,128)(2,1)} %reshape.29.scaled, bf16[64,1184]{1,0:T(8,128)(2,1)} %reshape.30.out_noise), custom_call_target="tpu_custom_call" | custom-call | tf_op jit(solution)/shard_map/pallas_call | solution.py:394
  106.3 1.2 %slice.3 = f32[1,1]{1,0:T(1,128)} slice(f32[8,128]{1,0:T(8,128)} %get-tuple-element.8), slice={[0:1], [0:1]} | slice | bytes 8 | tf_op jit(solution)/shard_map/slice | solution.py:432
  108.2 0.0 copy-done
  108.2 0.0 copy-start.1
  108.2 3.9 %add_convert_fusion = (bf16[448,1184]{1,0:T(8,128)(2,1)}, f32[448,1184]{1,0:T(8,128)}) fusion(bf16[448,1184]{1,0:T(8,128)(2,1)S(1)} %copy-done, f32[448,1184]{1,0:T(8,128)} %get-tuple-element.7, f32[]{:T(128)} %bitcast.3), kind=kLoop, calls=%fused_computation | loop fusion | flops 2652160 | bytes 6365188 | tf_op jit(solution)/shard_map/convert_element_type | solution.py:434
  112.1 0.0 copy-done.1
  112.1 1.5 %copy.12 = bf16[16,64,1184]{2,1,0:T(8,128)(2,1)} copy(bf16[16,64,1184]{2,1,0:T(8,128)(2,1)S(1)} %bitcast.6) | data formatting | bytes 4849664
Async XLA Ops:
  4.7 103.5 %copy-start = (bf16[448,1184]{1,0:T(8,128)(2,1)S(1)}, bf16[448,1184]{1,0:T(8,128)(2,1)}, u32[]{:S(2)}) copy-start(bf16[448,1184]{1,0:T(8,128)(2,1)} %weight.1) | copy-start | bytes 3182596
  108.2 3.9 %copy-start.1 = (bf16[1024,1184]{1,0:T(8,128)(2,1)S(1)}, bf16[1024,1184]{1,0:T(8,128)(2,1)}, u32[]{:S(2)}) copy-start(bf16[1024,1184]{1,0:T(8,128)(2,1)} %get-tuple-element.6) | copy-start | bytes 7274500

commit v2 on v1

v2 whole, which is shorter than its diff:
```python
import jax
import jax.numpy as jnp
from jax import lax
from jax.experimental import pallas as pl
from jax.experimental.pallas import tpu as pltpu
from jax.sharding import PartitionSpec as P

D = 3584
F = 18944
NX = 4
NZ = 4
POP = 8
COL = 16
MEMBERS = 16
ROWS = 448
WIDE = 1184
MAIN = 1152
REST = WIDE - MAIN
FEAT = 224
TOKENS = 1024
PART = 64
GROUPS = ((0, 256), (256, 256), (512, 256), (768, 256), (1024, 128))
NG = len(GROUPS)
TILE = 256
MESH = pl.DeviceIdType.MESH
BF16 = jnp.bfloat16
F32 = jnp.float32


def kernel(
    acts,
    weight,
    noise_in,
    out_in,
    ranks_in,
    out,
    step_out,
    new_out,
    wbuf,
    xbuf,
    abuf,
    bbuf,
    tbuf,
    ranks,
    noise_raw,
    out_raw,
    noise,
    out_noise,
    acc,
    low,
    delta,
    part,
    parts,
    wsem,
    bsem,
    tsem,
    asem,
    xsem,
    rsem,
    ssem,
    lsem,
):
    pop, col = lax.axis_index("pop"), lax.axis_index("col")
    x, ylo = pop % NX, pop // NX
    z, yhi, core = col // 4, (col // 2) % 2, col % 2
    mine = z * 2 + core

    def pop_at(dy, dx):
        return (ylo * (1 - 2 * dy) + dy) * NX + (x + dx) % NX

    def col_at(dz, dy, dc):
        return (
            ((z + dz) % NZ) * 4
            + (yhi * (1 - 2 * dy) + dy) * 2
            + (core * (1 - 2 * dc) + dc)
        )

    right, left = (pop_at(0, 1), col), (pop_at(0, 3), col)
    pair = (pop_at(1, 0), col)
    up, down = (pop, col_at(1, 0, 0)), (pop, col_at(3, 0, 0))
    far, twin = (pop, col_at(0, 1, 0)), (pop, col_at(0, 0, 1))
    pop_peers = [
        (dy * NX + dx, (pop_at(dy, dx), col))
        for dy in range(2)
        for dx in range(NX)
        if dy + dx > 0
    ]
    col_peers = [
        (dz * 2 + dc, (pop, col_at(dz, 0, dc)))
        for dz in range(NZ)
        for dc in range(2)
        if dz + dc > 0
    ]

    sent = []

    def send(src, dst, sem, device):
        copy = pltpu.make_async_remote_copy(
            src_ref=src,
            dst_ref=dst,
            send_sem=ssem.at[len(sent)],
            recv_sem=sem,
            device_id=device,
            device_id_type=MESH,
        )
        copy.start()
        sent.append(copy)

    def arrive(dst, sem):
        pltpu.make_async_remote_copy(
            src_ref=dst,
            dst_ref=dst,
            send_sem=ssem.at[0],
            recv_sem=sem,
            device_id=right,
            device_id_type=MESH,
        ).wait_recv()

    own_noise = pltpu.make_async_copy(noise_in, noise_raw, lsem.at[0])
    own_out = pltpu.make_async_copy(out_in, out_raw, lsem.at[1])
    own_weight = pltpu.make_async_copy(weight, wbuf.at[0], lsem.at[2])
    own_acts = pltpu.make_async_copy(acts, xbuf.at[col], lsem.at[3])
    own_ranks = pltpu.make_async_copy(ranks_in, ranks, lsem.at[6])
    for copy in (own_ranks, own_out, own_noise, own_weight, own_acts):
        copy.start()

    barrier = pltpu.get_barrier_semaphore()
    peers = [device for _, device in pop_peers + col_peers] + [far]
    for device in peers:
        pl.semaphore_signal(barrier, inc=1, device_id=device, device_id_type=MESH)
    pl.semaphore_wait(barrier, len(peers))

    def piece(h, j):
        return pl.ds(h * FEAT, FEAT), pl.ds(*GROUPS[j])

    def w_at(slot, h, j):
        r, c = piece(h, j)
        return wbuf.at[slot, r, c]

    def w_send(src_slot, h, j, dst_slot, device):
        r, c = piece(h, j)
        src = weight.at[r, c] if src_slot == 0 else wbuf.at[src_slot, r, c]
        send(src, w_at(dst_slot, h, j), wsem.at[(dst_slot * 2 + h) * NG + j], device)

    def w_arrive(slot, h, j):
        arrive(w_at(slot, h, j), wsem.at[(slot * 2 + h) * NG + j])

    def b_at(slot, k):
        return bbuf.at[pl.ds(slot * PART + k * 32, 32), pl.ds(0, MAIN)]

    def t_at(slot, k):
        return tbuf.at[slot, pl.ds(k * 64, 64), :]

    def b_send(src_slot, k, dst_slot, device):
        send(b_at(src_slot, k), b_at(dst_slot, k), bsem.at[dst_slot * 2 + k], device)
        send(t_at(src_slot, k), t_at(dst_slot, k), tsem.at[dst_slot * 2 + k], device)

    def b_arrive(slot, k):
        arrive(b_at(slot, k), bsem.at[slot * 2 + k])
        arrive(t_at(slot, k), tsem.at[slot * 2 + k])

    def x_at(c, half=None):
        if half is None:
            return xbuf.at[c]
        return xbuf.at[c, pl.ds(half * (TOKENS // 2), TOKENS // 2), :]

    def x_send(c, half, sem, device, src=None):
        send(x_at(c, half) if src is None else src, x_at(c, half), xsem.at[sem], device)

    def x_arrive(c, half, sem):
        arrive(x_at(c, half), xsem.at[sem])

    to_right = [(h, j) for h in (0, 1) for j in range(NG)]
    to_left = [(h, j) for h in (1, 0) for j in range(NG)]
    to_pair = [(h, j) for j in range(NG) for h in (0, 1)]

    def own_pieces(first, last):
        for i in range(first, last):
            w_send(0, *to_right[i], 3, right)
            w_send(0, *to_left[i], 1, left)

    def own_to_pair(first, last):
        for i in range(first, last):
            w_send(0, *to_pair[i], 4, pair)

    x_send(col, None, 0, up, acts)
    x_send(col, None, 1, down, acts)
    own_pieces(0, 2)
    own_to_pair(0, 2)
    x_send(col, None, 2, far, acts)
    x_send(col, None, 9, twin, acts)

    own_ranks.wait()
    own_out.wait()
    raw = jnp.concatenate([out_raw[m].astype(F32) for m in range(MEMBERS)], axis=0)
    out_noise[...] = raw.astype(BF16)
    fit = jnp.concatenate(
        [
            jnp.full((4, 1), ranks[m].astype(F32), F32) / (MEMBERS * POP - 1) - 0.5
            for m in range(MEMBERS)
        ],
        axis=0,
    )
    scaled = raw * fit
    bbuf[pl.ds(0, PART), :] = scaled.astype(BF16)
    own_weight.wait()
    last = wbuf[0, :, pl.ds(MAIN, REST)].astype(F32)
    tbuf[0, pl.ds(0, 112), :] = jnp.concatenate(
        [last[g * 112 : g * 112 + 112] for g in range(4)], axis=1
    ).astype(BF16)
    tbuf[0, pl.ds(112, 16), :] = jnp.concatenate(
        [scaled[g * 16 : g * 16 + 16, MAIN:WIDE] for g in range(4)], axis=1
    ).astype(BF16)
    own_noise.wait()
    wide = jnp.concatenate([noise_raw[m].astype(F32) for m in range(MEMBERS)], axis=0)
    for c in range(COL):
        noise[c] = wide[:, c * FEAT : (c + 1) * FEAT].astype(BF16)

    for k, device, slot in ((0, right, 3), (1, left, 1), (0, pair, 4), (1, right, 3), (0, left, 1), (1, pair, 4)):
        b_send(0, k, slot, device)

    def a_at(slot):
        return abuf.at[:, pl.ds(slot * PART, PART), :]

    target = (ylo + mine // NX) % 2 * NX + (x + NX - mine % NX) % NX
    fetch = pltpu.make_async_remote_copy(
        src_ref=noise.at[pl.ds(2 * target, 2)],
        dst_ref=a_at(mine),
        send_sem=lsem.at[4],
        recv_sem=asem.at[0],
        device_id=(target, col),
        device_id_type=MESH,
    )
    keep = pltpu.make_async_copy(noise.at[pl.ds(2 * pop, 2)], a_at(0), lsem.at[5])

    @pl.when(mine > 0)
    def _():
        fetch.start()

    @pl.when(mine == 0)
    def _():
        keep.start()

    own_pieces(2, 6)
    own_to_pair(2, 7)

    c_down, c_up = col_at(3, 0, 0), col_at(1, 0, 0)
    c_far, c_opp = col_at(0, 1, 0), col_at(2, 0, 0)
    f_down, f_up, f_opp = col_at(3, 1, 0), col_at(1, 1, 0), col_at(2, 1, 0)

    def add_low(c):
        low[...] += lax.dot_general(
            xbuf[c],
            noise[c],
            (((1,), (1,)), ((), ())),
            preferred_element_type=F32,
        )

    low[...] = jnp.zeros_like(low)
    own_acts.wait()
    add_low(col)

    x_arrive(c_down, None, 0)
    x_send(c_down, 0, 5, up)
    x_send(c_down, None, 10, twin)
    x_arrive(c_up, None, 1)
    x_send(c_up, 1, 6, down)
    x_send(c_up, None, 11, twin)

    b_arrive(3, 0)
    b_send(3, 0, 2, right)
    b_arrive(1, 1)
    b_send(1, 1, 2, left)
    for k in range(2):
        b_arrive(4, k)
        b_send(4, k, 7, right)
        b_send(4, k, 5, left)
    own_pieces(6, 10)

    @pl.when(mine > 0)
    def _():
        fetch.wait()

    @pl.when(mine == 0)
    def _():
        keep.wait()

    for i, device in col_peers:
        send(a_at(mine), a_at(mine), asem.at[i], device)

    add_low(c_down)
    add_low(c_up)
    x_arrive(c_far, None, 2)
    x_send(c_far, None, 3, up)
    x_send(c_far, None, 4, down)
    x_send(c_far, None, 12, twin)
    for k in range(2):
        b_arrive(2, k)
        b_send(2, k, 6, pair)
    own_to_pair(7, 10)
    add_low(c_far)

    for j in range(NG):
        w_arrive(3, 0, j)
        w_send(3, 0, j, 2, right)
        w_arrive(1, 1, j)
        w_send(1, 1, j, 2, left)

    b_arrive(3, 1)
    b_arrive(1, 0)
    for slot in (7, 5, 6):
        for k in range(2):
            b_arrive(slot, k)
    for i, _ in col_peers:
        dz, dc = i // 2, i % 2
        sender = ((z + NZ - dz) % NZ) * 2 + (core * (1 - 2 * dc) + dc)
        arrive(a_at(sender), asem.at[i])

    @pl.loop(1, POP)
    def _(slot):
        packed = tbuf[slot].astype(F32)
        for g in range(4):
            mid = packed[:, g * REST : (g + 1) * REST].astype(BF16)
            wbuf[slot, pl.ds(g * 112, 112), pl.ds(MAIN, REST)] = mid[:112]
            bbuf[
                pl.ds(pl.multiple_of(slot * PART + g * 16, 16), 16), pl.ds(MAIN, REST)
            ] = mid[112:]

    squares = jnp.zeros((), F32)
    for h in range(2):
        block = lax.dot_general(
            abuf[h], bbuf[...], (((0,), (0,)), ((), ())), preferred_element_type=F32
        )
        delta[pl.ds(h * FEAT, FEAT), :] = block
        squares += jnp.sum(block * block)
    part[0] = jnp.full((8, 128), squares, F32)

    x_arrive(f_down, None, 3)
    x_send(f_down, 0, 7, up)
    x_send(f_down, None, 13, twin)
    x_arrive(f_up, None, 4)
    x_send(f_up, 1, 8, down)
    x_send(f_up, None, 14, twin)

    for i, device in col_peers:
        send(part.at[0], parts.at[i], rsem.at[i], device)
    add_low(f_down)
    add_low(f_up)

    for j in range(2):
        w_arrive(2, 0, j)
        w_send(2, 0, j, 6, pair)
        w_arrive(2, 1, j)
        w_send(2, 1, j, 6, pair)

    for i, _ in col_peers:
        arrive(parts.at[i], rsem.at[i])
    total = part[0]
    for i, _ in col_peers:
        total = total + parts[i]
    part[1] = total

    x_arrive(c_opp, 0, 5)
    x_send(c_opp, 0, 15, twin)
    x_arrive(c_opp, 1, 6)
    x_send(c_opp, 1, 16, twin)
    send(part.at[1], parts.at[8], rsem.at[8], far)
    add_low(c_opp)
    x_arrive(f_opp, 0, 7)
    x_send(f_opp, 0, 17, twin)
    x_arrive(f_opp, 1, 8)
    x_send(f_opp, 1, 18, twin)
    add_low(f_opp)

    def pass_on(first, last):
        for i in range(first, last):
            h, j = to_pair[i]
            w_arrive(4, h, j)
            w_send(4, h, j, 7, right)
            w_send(4, h, j, 5, left)

    pass_on(0, 2)
    for (dz, dy), sems in (
        ((0, 0), ((None, 9),)),
        ((3, 0), ((None, 10),)),
        ((1, 0), ((None, 11),)),
        ((0, 1), ((None, 12),)),
        ((3, 1), ((None, 13),)),
        ((1, 1), ((None, 14),)),
        ((2, 0), ((0, 15), (1, 16))),
        ((2, 1), ((0, 17), (1, 18))),
    ):
        c = col_at(dz, dy, 1)
        for half, sem in sems:
            x_arrive(c, half, sem)
        add_low(c)
    for j in range(2, NG):
        w_arrive(2, 0, j)
        w_send(2, 0, j, 6, pair)
        w_arrive(2, 1, j)
        w_send(2, 1, j, 6, pair)

    arrive(parts.at[8], rsem.at[8])
    part[2] = part[1] + parts[8]
    pass_on(2, 3)

    rank = lax.broadcasted_iota(jnp.int32, (TOKENS, PART), 1) // 4
    token = lax.broadcasted_iota(jnp.int32, (TOKENS, PART), 0) // 64
    low[...] = jnp.where(rank == token, low[...] * 0.5, 0.0)

    def rows(i):
        return pl.ds(pl.multiple_of(i * TILE, TILE), TILE)

    @pl.loop(0, TOKENS // TILE)
    def _(i):
        left_over = low[rows(i), :]
        value = None
        for _ in range(3):
            term = left_over.astype(BF16)
            left_over = left_over - term.astype(F32)
            product = jnp.dot(term, out_noise[...], preferred_element_type=F32)
            value = product if value is None else value + product
        acc[rows(i), :] = value

    for i, device in pop_peers:
        send(part.at[2], parts.at[8 + i], rsem.at[8 + i], device)
    pass_on(3, 5)

    def dot(i, slot, h, cols):
        c = 2 * pop_at(slot // NX, slot % NX) + h
        return jnp.dot(
            xbuf[c, rows(i), :],
            wbuf[slot, pl.ds(h * FEAT, FEAT), cols],
            preferred_element_type=F32,
        )

    everything = pl.ds(0, WIDE)

    def blocks(slot):
        @pl.loop(0, TOKENS // TILE)
        def _(i):
            for h in range(2):
                acc[rows(i), :] += dot(i, slot, h, everything)

    blocks(0)
    pass_on(5, 7)
    for j in range(NG):
        w_arrive(3, 1, j)
        w_arrive(1, 0, j)
    blocks(1)
    pass_on(7, 9)
    blocks(3)
    pass_on(9, 10)
    blocks(4)
    blocks(2)

    total = part[2]
    for i, _ in pop_peers:
        arrive(parts.at[8 + i], rsem.at[8 + i])
        total = total + parts[8 + i]
    scale = lax.rsqrt(total / (D * F) + 1e-06)[0:1, 0:1]
    step = delta[...] * scale
    step_out[...] = step
    new_out[...] = (wbuf[0].astype(F32) + 0.01 * step).astype(BF16)
    for j in range(NG):
        for h in range(2):
            for slot in (5, 7, 6):
                w_arrive(slot, h, j)
        first, n = GROUPS[j]
        cols = pl.ds(first, n if j < NG - 1 else WIDE - first)

        @pl.loop(0, TOKENS // TILE)
        def _(i):
            value = acc[rows(i), cols]
            for slot in (5, 7, 6):
                for h in range(2):
                    value = value + dot(i, slot, h, cols)
            out[rows(i), cols] = value.astype(BF16)


    for copy in sent:
        copy.wait_send()


def put_out(out_v, step_v, new_v, out, step_out, new_out, sem):
    writes = [
        pltpu.make_async_copy(src, dst, sem.at[i])
        for i, (src, dst) in enumerate(
            ((step_v, step_out), (out_v, out), (new_v, new_out))
        )
    ]
    for copy in writes:
        copy.start()
    for copy in writes:
        copy.wait()


def body(acts, weight, input_noise_factor, output_noise_factor, ranks):
    hbm = pl.BlockSpec(memory_space=pltpu.HBM)
    vmem = pl.BlockSpec(memory_space=pltpu.VMEM)
    made = pl.pallas_call(
        kernel,
        out_shape=(
            pltpu.VMEM((TOKENS, WIDE), BF16),
            pltpu.VMEM((ROWS, WIDE), F32),
            pltpu.VMEM((ROWS, WIDE), BF16),
        ),
        in_specs=[hbm] * 5,
        out_specs=(vmem,) * 3,
        scratch_shapes=[
            pltpu.VMEM((POP, ROWS, WIDE), BF16),
            pltpu.VMEM((COL, TOKENS, FEAT), BF16),
            pltpu.VMEM((2, POP * PART, FEAT), BF16),
            pltpu.VMEM((POP * PART, WIDE), BF16),
            pltpu.VMEM((POP, 128, 128), BF16),
            pltpu.SMEM((MEMBERS,), jnp.int32),
            pltpu.VMEM((MEMBERS, 4, D), BF16),
            pltpu.VMEM((MEMBERS, 4, WIDE), BF16),
            pltpu.VMEM((COL, PART, FEAT), BF16),
            pltpu.VMEM((PART, WIDE), BF16),
            pltpu.VMEM((TOKENS, WIDE), F32),
            pltpu.VMEM((TOKENS, PART), F32),
            pltpu.VMEM((ROWS, WIDE), F32),
            pltpu.VMEM((3, 8, 128), F32),
            pltpu.VMEM((16, 8, 128), F32),
            pltpu.SemaphoreType.DMA((POP * 2 * NG,)),
            pltpu.SemaphoreType.DMA((POP * 2,)),
            pltpu.SemaphoreType.DMA((POP * 2,)),
            pltpu.SemaphoreType.DMA((8,)),
            pltpu.SemaphoreType.DMA((19,)),
            pltpu.SemaphoreType.DMA((16,)),
            pltpu.SemaphoreType.DMA((192,)),
            pltpu.SemaphoreType.DMA((13,)),
        ],
        compiler_params=pltpu.CompilerParams(
            collective_id=0, has_side_effects=True, vmem_limit_bytes=57 * 1024 * 1024
        ),
    )(
        acts.reshape(TOKENS, FEAT),
        weight,
        input_noise_factor,
        output_noise_factor,
        pltpu.with_memory_space_constraint(ranks, pltpu.HBM),
    )
    out, step_dir, new_weight = pl.pallas_call(
        put_out,
        out_shape=(
            jax.ShapeDtypeStruct((TOKENS, WIDE), BF16),
            jax.ShapeDtypeStruct((ROWS, WIDE), F32),
            jax.ShapeDtypeStruct((ROWS, WIDE), BF16),
        ),
        in_specs=[vmem] * 3,
        out_specs=(hbm,) * 3,
        scratch_shapes=[pltpu.SemaphoreType.DMA((3,))],
        compiler_params=pltpu.CompilerParams(vmem_limit_bytes=16 * 1024 * 1024),
    )(*made)
    return (out.reshape(MEMBERS, TOKENS // MEMBERS, WIDE), step_dir, new_weight)


def solution(mesh):
    in_specs = (
        P("pop", None, "col"),
        P("pop", "col"),
        P("pop", None, None),
        P("pop", None, "col"),
        P("pop"),
    )
    out_specs = (P("pop", None, "col"), P("pop", "col"), P("pop", "col"))
    return jax.shard_map(body, mesh=mesh, in_specs=in_specs, out_specs=out_specs, check_vma=False)
```

time: 116 us -> 90.4 us (0.78); the launches traced: 114 us -> 90.2 us
  Pallas kernels: 98.8 us -> 89.6 us
  local copies, waits for them, and re-layouts: 7.83 us -> 0 us
  other arithmetic: 5.59 us -> 0 us
    pallas_call x1 -> x2, Pallas kernels: 98.8 us -> 89.6 us  [the longest x1 87 us: body(): pl.pallas_call(kernel, out_shape=(pltpu.VMEM((TOKENS, WIDE), BF16), pltpu...]
    reshape x4 -> x0, local copies, waits for them, and re-layouts: 5.14 us -> none  [the longest x2 2.79 us: body(): noise = input_noise_factor.reshape(PART, COL, FEAT).transpose(1, 0, 2)]
    convert_element_type x2 -> x0, other arithmetic: 4.93 us -> none  [the longest x1 3.89 us: body(): new_weight = (weight.astype(F32) + 0.01 * step_dir).astype(BF16)]
    unnamed x5 -> x0, local copies, waits for them, and re-layouts: 1.5 us -> none
    slice x1 -> x0, local copies, waits for them, and re-layouts: 1.19 us -> none  [body(): mean_sq = total[0, 0] / (D * F)]
where the time goes in v2:
time: 90.4 us; the launch traced here: 90.2 us
  Pallas kernels  89.6 us (99%)
    pallas_call x1, Pallas kernels, body(): pl.pallas_call(kernel, out_shape=(pltpu.VMEM((TOKENS, WIDE), BF16), pltpu...  87 us
    pallas_call x1, Pallas kernels, body(): pl.pallas_call(put_out, out_shape=(jax.ShapeDtypeStruct((TOKENS, WIDE), B...  2.65 us

profile of v2, /device:TPU:1, one launch (start us, length us, event | category | flops | bytes accessed | tf_op | source)
XLA Modules:
  0.0 90.2 jit_solution(3773200361882758108)
XLA Ops:
  0.6 87.0 %shard_map.76 = (bf16[1024,1184]{1,0:T(8,128)(2,1)S(1)}, f32[448,1184]{1,0:T(8,128)S(1)}, bf16[448,1184]{1,0:T(8,128)(2,1)S(1)}) custom-call(bf16[1024,224]{1,0:T(8,128)(2,1)} %bitcast.2, bf16[448,1184]{1,0:T(8,128)(2,1)} %weight.1, bf16[16,4,3584]{2,1,0:T(4,128)(2,1)} %noise_in.1, bf16[16,4,1184]{2,1,0:T(4,128)(2,1)} %out_in.1, s32[16]{0:T(128)} %ranks_in.1), custom_call_target="tpu_custom_call" | custom-call | tf_op jit(solution)/shard_map/pallas_call | solution.py:501
  87.6 2.6 %shard_map.77 = (bf16[1024,1184]{1,0:T(8,128)(2,1)}, f32[448,1184]{1,0:T(8,128)}, bf16[448,1184]{1,0:T(8,128)(2,1)}) custom-call(bf16[1024,1184]{1,0:T(8,128)(2,1)S(1)} %get-tuple-element.9.out_v, f32[448,1184]{1,0:T(8,128)S(1)} %get-tuple-element.10.step_v, bf16[448,1184]{1,0:T(8,128)(2,1)S(1)} %get-tuple-element.11.new_v), custom_call_target="tpu_custom_call" | custom-call | tf_op jit(solution)/shard_map/pallas_call | solution.py:545

commit v3 on v2

--- a/solution.py
+++ b/solution.py
@@ -186,8 +186,7 @@
     x_send(col, None, 0, up, acts)
     x_send(col, None, 1, down, acts)
     own_pieces(0, 2)
-    own_to_pair(0, 2)
-    x_send(col, None, 2, far, acts)
+    own_to_pair(0, 1)
     x_send(col, None, 9, twin, acts)
 
     own_ranks.wait()
@@ -241,8 +240,8 @@
     def _():
         keep.start()
 
-    own_pieces(2, 6)
-    own_to_pair(2, 7)
+    x_send(col, None, 2, far, acts)
+    own_pieces(2, 4)
 
     c_down, c_up = col_at(3, 0, 0), col_at(1, 0, 0)
     c_far, c_opp = col_at(0, 1, 0), col_at(2, 0, 0)
@@ -256,16 +255,25 @@
             preferred_element_type=F32,
         )
 
-    low[...] = jnp.zeros_like(low)
-    own_acts.wait()
-    add_low(col)
-
-    x_arrive(c_down, None, 0)
-    x_send(c_down, 0, 5, up)
-    x_send(c_down, None, 10, twin)
-    x_arrive(c_up, None, 1)
-    x_send(c_up, 1, 6, down)
-    x_send(c_up, None, 11, twin)
+    def relay(first, last):
+        for j in range(first, last):
+            w_arrive(3, 0, j)
+            w_send(3, 0, j, 2, right)
+            w_arrive(1, 1, j)
+            w_send(1, 1, j, 2, left)
+
+    def across(first, last):
+        for j in range(first, last):
+            for h in range(2):
+                w_arrive(2, h, j)
+                w_send(2, h, j, 6, pair)
+
+    def pass_on(first, last):
+        for i in range(first, last):
+            h, j = to_pair[i]
+            w_arrive(4, h, j)
+            w_send(4, h, j, 7, right)
+            w_send(4, h, j, 5, left)
 
     b_arrive(3, 0)
     b_send(3, 0, 2, right)
@@ -275,7 +283,18 @@
         b_arrive(4, k)
         b_send(4, k, 7, right)
         b_send(4, k, 5, left)
-    own_pieces(6, 10)
+    own_pieces(4, 7)
+
+    low[...] = jnp.zeros_like(low)
+    own_acts.wait()
+    add_low(col)
+
+    x_arrive(c_down, None, 0)
+    x_send(c_down, 0, 5, up)
+    x_send(c_down, None, 10, twin)
+    x_arrive(c_up, None, 1)
+    x_send(c_up, 1, 6, down)
+    x_send(c_up, None, 11, twin)
 
     @pl.when(mine > 0)
     def _():
@@ -285,36 +304,37 @@
     def _():
         keep.wait()
 
-    for i, device in col_peers:
-        send(a_at(mine), a_at(mine), asem.at[i], device)
-
+    for dz, device in ((1, up), (3, down), (2, (pop, col_at(2, 0, 0)))):
+        send(a_at(mine), a_at(mine), asem.at[2 * dz], device)
+    send(a_at(mine), a_at(mine), asem.at[1], twin)
+
+    for k in range(2):
+        b_arrive(2, k)
+        b_send(2, k, 6, pair)
+    own_to_pair(1, 5)
     add_low(c_down)
     add_low(c_up)
     x_arrive(c_far, None, 2)
     x_send(c_far, None, 3, up)
     x_send(c_far, None, 4, down)
     x_send(c_far, None, 12, twin)
-    for k in range(2):
-        b_arrive(2, k)
-        b_send(2, k, 6, pair)
-    own_to_pair(7, 10)
+    own_pieces(7, 9)
     add_low(c_far)
-
-    for j in range(NG):
-        w_arrive(3, 0, j)
-        w_send(3, 0, j, 2, right)
-        w_arrive(1, 1, j)
-        w_send(1, 1, j, 2, left)
 
     b_arrive(3, 1)
     b_arrive(1, 0)
     for slot in (7, 5, 6):
         for k in range(2):
             b_arrive(slot, k)
-    for i, _ in col_peers:
-        dz, dc = i // 2, i % 2
-        sender = ((z + NZ - dz) % NZ) * 2 + (core * (1 - 2 * dc) + dc)
-        arrive(a_at(sender), asem.at[i])
+    def owner(dz, dc):
+        return ((z + NZ - dz) % NZ) * 2 + (core * (1 - 2 * dc) + dc)
+
+    for dz in (1, 3, 2):
+        block = a_at(owner(dz, 0))
+        arrive(block, asem.at[2 * dz])
+        send(block, block, asem.at[2 * dz + 1], twin)
+    for dz in range(NZ):
+        arrive(a_at(owner(dz, 1)), asem.at[2 * dz + 1])
 
     @pl.loop(1, POP)
     def _(slot):
@@ -335,74 +355,62 @@
         squares += jnp.sum(block * block)
     part[0] = jnp.full((8, 128), squares, F32)
 
+    for i, device in pop_peers:
+        send(part.at[0], parts.at[8 + i], rsem.at[8 + i], device)
+    own_pieces(9, 10)
+    own_to_pair(5, 8)
+    relay(0, NG)
+    x_arrive(c_opp, 0, 5)
+    x_send(c_opp, 0, 15, twin)
+    x_arrive(c_opp, 1, 6)
+    x_send(c_opp, 1, 16, twin)
+    add_low(c_opp)
     x_arrive(f_down, None, 3)
     x_send(f_down, 0, 7, up)
     x_send(f_down, None, 13, twin)
     x_arrive(f_up, None, 4)
     x_send(f_up, 1, 8, down)
     x_send(f_up, None, 14, twin)
-
-    for i, device in col_peers:
-        send(part.at[0], parts.at[i], rsem.at[i], device)
+    total = part[0]
+    for i, _ in pop_peers:
+        arrive(parts.at[8 + i], rsem.at[8 + i])
+        total = total + parts[8 + i]
+    part[1] = total
     add_low(f_down)
     add_low(f_up)
-
-    for j in range(2):
-        w_arrive(2, 0, j)
-        w_send(2, 0, j, 6, pair)
-        w_arrive(2, 1, j)
-        w_send(2, 1, j, 6, pair)
-
-    for i, _ in col_peers:
-        arrive(parts.at[i], rsem.at[i])
-    total = part[0]
-    for i, _ in col_peers:
-        total = total + parts[i]
-    part[1] = total
-
-    x_arrive(c_opp, 0, 5)
-    x_send(c_opp, 0, 15, twin)
-    x_arrive(c_opp, 1, 6)
-    x_send(c_opp, 1, 16, twin)
     send(part.at[1], parts.at[8], rsem.at[8], far)
-    add_low(c_opp)
+    own_to_pair(8, 10)
+    across(0, 1)
+    pass_on(0, 4)
+
+    def add_twin(dz, dy, *sems):
+        c = col_at(dz, dy, 1)
+        for i, sem in enumerate(sems):
+            x_arrive(c, i if len(sems) > 1 else None, sem)
+        add_low(c)
+
+    add_twin(0, 0, 9)
+    add_twin(3, 0, 10)
+    across(1, 2)
+    add_twin(1, 0, 11)
+    add_twin(0, 1, 12)
+    arrive(parts.at[8], rsem.at[8])
+    part[2] = part[1] + parts[8]
+    add_twin(2, 0, 15, 16)
+    across(2, 3)
+    for i, device in col_peers:
+        send(part.at[2], parts.at[i], rsem.at[i], device)
     x_arrive(f_opp, 0, 7)
     x_send(f_opp, 0, 17, twin)
     x_arrive(f_opp, 1, 8)
     x_send(f_opp, 1, 18, twin)
     add_low(f_opp)
-
-    def pass_on(first, last):
-        for i in range(first, last):
-            h, j = to_pair[i]
-            w_arrive(4, h, j)
-            w_send(4, h, j, 7, right)
-            w_send(4, h, j, 5, left)
-
-    pass_on(0, 2)
-    for (dz, dy), sems in (
-        ((0, 0), ((None, 9),)),
-        ((3, 0), ((None, 10),)),
-        ((1, 0), ((None, 11),)),
-        ((0, 1), ((None, 12),)),
-        ((3, 1), ((None, 13),)),
-        ((1, 1), ((None, 14),)),
-        ((2, 0), ((0, 15), (1, 16))),
-        ((2, 1), ((0, 17), (1, 18))),
-    ):
-        c = col_at(dz, dy, 1)
-        for half, sem in sems:
-            x_arrive(c, half, sem)
-        add_low(c)
-    for j in range(2, NG):
-        w_arrive(2, 0, j)
-        w_send(2, 0, j, 6, pair)
-        w_arrive(2, 1, j)
-        w_send(2, 1, j, 6, pair)
-
-    arrive(parts.at[8], rsem.at[8])
-    part[2] = part[1] + parts[8]
-    pass_on(2, 3)
+    add_twin(3, 1, 13)
+    add_twin(1, 1, 14)
+    across(3, 4)
+    add_twin(2, 1, 17, 18)
+    pass_on(4, 5)
+    across(4, NG)
 
     rank = lax.broadcasted_iota(jnp.int32, (TOKENS, PART), 1) // 4
     token = lax.broadcasted_iota(jnp.int32, (TOKENS, PART), 0) // 64
@@ -422,9 +430,7 @@
             value = product if value is None else value + product
         acc[rows(i), :] = value
 
-    for i, device in pop_peers:
-        send(part.at[2], parts.at[8 + i], rsem.at[8 + i], device)
-    pass_on(3, 5)
+    pass_on(5, 6)
 
     def dot(i, slot, h, cols):
         c = 2 * pop_at(slot // NX, slot % NX) + h
@@ -443,7 +449,7 @@
                 acc[rows(i), :] += dot(i, slot, h, everything)
 
     blocks(0)
-    pass_on(5, 7)
+    pass_on(6, 7)
     for j in range(NG):
         w_arrive(3, 1, j)
         w_arrive(1, 0, j)
@@ -455,9 +461,9 @@
     blocks(2)
 
     total = part[2]
-    for i, _ in pop_peers:
-        arrive(parts.at[8 + i], rsem.at[8 + i])
-        total = total + parts[8 + i]
+    for i, _ in col_peers:
+        arrive(parts.at[i], rsem.at[i])
+        total = total + parts[i]
     scale = lax.rsqrt(total / (D * F) + 1e-06)[0:1, 0:1]
     step = delta[...] * scale
     step_out[...] = step

time: 90.4 us -> 82.3 us (0.910)
  Pallas kernels: 89.6 us -> 81.6 us
    pallas_call x1, Pallas kernels: 87 us -> 78.9 us  [body(): pl.pallas_call(kernel, out_shape=(pltpu.VMEM((TOKENS, WIDE), BF16), pltpu...]
where the time goes in v3:
time: 82.3 us; the launch traced here: 82.2 us
  Pallas kernels  81.6 us (99%)
    pallas_call x1, Pallas kernels, body(): pl.pallas_call(kernel, out_shape=(pltpu.VMEM((TOKENS, WIDE), BF16), pltpu...  78.9 us
    pallas_call x1, Pallas kernels, body(): pl.pallas_call(put_out, out_shape=(jax.ShapeDtypeStruct((TOKENS, WIDE), B...  2.65 us

profile of v3, /device:TPU:1, one launch (start us, length us, event | category | flops | bytes accessed | tf_op | source)
XLA Modules:
  0.0 82.2 jit_solution(18335593291434313988)
XLA Ops:
  0.6 78.9 %shard_map.76 = (bf16[1024,1184]{1,0:T(8,128)(2,1)S(1)}, f32[448,1184]{1,0:T(8,128)S(1)}, bf16[448,1184]{1,0:T(8,128)(2,1)S(1)}) custom-call(bf16[1024,224]{1,0:T(8,128)(2,1)} %bitcast.2, bf16[448,1184]{1,0:T(8,128)(2,1)} %weight.1, bf16[16,4,3584]{2,1,0:T(4,128)(2,1)} %noise_in.1, bf16[16,4,1184]{2,1,0:T(4,128)(2,1)} %out_in.1, s32[16]{0:T(128)} %ranks_in.1), custom_call_target="tpu_custom_call" | custom-call | tf_op jit(solution)/shard_map/pallas_call | solution.py:507
  79.6 2.6 %shard_map.77 = (bf16[1024,1184]{1,0:T(8,128)(2,1)}, f32[448,1184]{1,0:T(8,128)}, bf16[448,1184]{1,0:T(8,128)(2,1)}) custom-call(bf16[1024,1184]{1,0:T(8,128)(2,1)S(1)} %get-tuple-element.9.out_v, f32[448,1184]{1,0:T(8,128)S(1)} %get-tuple-element.10.step_v, bf16[448,1184]{1,0:T(8,128)(2,1)S(1)} %get-tuple-element.11.new_v), custom_call_target="tpu_custom_call" | custom-call | tf_op jit(solution)/shard_map/pallas_call | solution.py:551

commit v4 on v3

--- a/solution.py
+++ b/solution.py
@@ -38,6 +38,7 @@
     new_out,
     wbuf,
     xbuf,
+    acc,
     abuf,
     bbuf,
     tbuf,
@@ -46,7 +47,6 @@
     out_raw,
     noise,
     out_noise,
-    acc,
     low,
     delta,
     part,
@@ -472,8 +472,9 @@
         for h in range(2):
             for slot in (5, 7, 6):
                 w_arrive(slot, h, j)
-        first, n = GROUPS[j]
-        cols = pl.ds(first, n if j < NG - 1 else WIDE - first)
+        if j == NG - 1:
+            break
+        cols = pl.ds(*GROUPS[j])
 
         @pl.loop(0, TOKENS // TILE)
         def _(i):
@@ -488,15 +489,41 @@
         copy.wait_send()
 
 
-def put_out(out_v, step_v, new_v, out, step_out, new_out, sem):
+def put_out(
+    out_v, step_v, new_v, wbuf, xbuf, acc, out, step_out, new_out, last, sem
+):
+    first = GROUPS[-1][0]
+    cols = pl.ds(first, WIDE - first)
+    ready = pl.ds(0, first)
+    pairs = (
+        (step_v, step_out),
+        (out_v.at[:, ready], out.at[:, ready]),
+        (new_v, new_out),
+        (last, out.at[:, cols]),
+    )
     writes = [
-        pltpu.make_async_copy(src, dst, sem.at[i])
-        for i, (src, dst) in enumerate(
-            ((step_v, step_out), (out_v, out), (new_v, new_out))
-        )
+        pltpu.make_async_copy(src, dst, sem.at[i]) for i, (src, dst) in enumerate(pairs)
     ]
-    for copy in writes:
+    for copy in writes[:3]:
         copy.start()
+    pop = lax.axis_index("pop")
+    x, ylo = pop % NX, pop // NX
+
+    @pl.loop(0, TOKENS // TILE)
+    def _(i):
+        rows = pl.ds(pl.multiple_of(i * TILE, TILE), TILE)
+        value = acc[rows, cols]
+        for slot in (5, 7, 6):
+            source = (1 - ylo) * NX + (x + slot % NX) % NX
+            for h in range(2):
+                value = value + jnp.dot(
+                    xbuf[2 * source + h, rows, :],
+                    wbuf[slot, pl.ds(h * FEAT, FEAT), cols],
+                    preferred_element_type=F32,
+                )
+        last[rows, :] = value.astype(BF16)
+
+    writes[3].start()
     for copy in writes:
         copy.wait()
 
@@ -510,12 +537,13 @@
             pltpu.VMEM((TOKENS, WIDE), BF16),
             pltpu.VMEM((ROWS, WIDE), F32),
             pltpu.VMEM((ROWS, WIDE), BF16),
+            pltpu.VMEM((POP, ROWS, WIDE), BF16),
+            pltpu.VMEM((COL, TOKENS, FEAT), BF16),
+            pltpu.VMEM((TOKENS, WIDE), F32),
         ),
         in_specs=[hbm] * 5,
-        out_specs=(vmem,) * 3,
+        out_specs=(vmem,) * 6,
         scratch_shapes=[
-            pltpu.VMEM((POP, ROWS, WIDE), BF16),
-            pltpu.VMEM((COL, TOKENS, FEAT), BF16),
             pltpu.VMEM((2, POP * PART, FEAT), BF16),
             pltpu.VMEM((POP * PART, WIDE), BF16),
             pltpu.VMEM((POP, 128, 128), BF16),
@@ -524,7 +552,6 @@
             pltpu.VMEM((MEMBERS, 4, WIDE), BF16),
             pltpu.VMEM((COL, PART, FEAT), BF16),
             pltpu.VMEM((PART, WIDE), BF16),
-            pltpu.VMEM((TOKENS, WIDE), F32),
             pltpu.VMEM((TOKENS, PART), F32),
             pltpu.VMEM((ROWS, WIDE), F32),
             pltpu.VMEM((3, 8, 128), F32),
@@ -539,7 +566,7 @@
             pltpu.SemaphoreType.DMA((13,)),
         ],
         compiler_params=pltpu.CompilerParams(
-            collective_id=0, has_side_effects=True, vmem_limit_bytes=57 * 1024 * 1024
+            collective_id=0, has_side_effects=True, vmem_limit_bytes=34 * 1024 * 1024
         ),
     )(
         acts.reshape(TOKENS, FEAT),
@@ -555,10 +582,13 @@
             jax.ShapeDtypeStruct((ROWS, WIDE), F32),
             jax.ShapeDtypeStruct((ROWS, WIDE), BF16),
         ),
-        in_specs=[vmem] * 3,
+        in_specs=[vmem] * 6,
         out_specs=(hbm,) * 3,
-        scratch_shapes=[pltpu.SemaphoreType.DMA((3,))],
-        compiler_params=pltpu.CompilerParams(vmem_limit_bytes=16 * 1024 * 1024),
+        scratch_shapes=[
+            pltpu.VMEM((TOKENS, WIDE - GROUPS[-1][0]), BF16),
+            pltpu.SemaphoreType.DMA((4,)),
+        ],
+        compiler_params=pltpu.CompilerParams(vmem_limit_bytes=4 * 1024 * 1024),
     )(*made)
     return (out.reshape(MEMBERS, TOKENS // MEMBERS, WIDE), step_dir, new_weight)
 

time: 82.3 us -> 80.9 us (0.983)
  Pallas kernels: 81.6 us -> 80.2 us
    pallas_call x1, Pallas kernels: 78.9 us -> 77.6 us  [body(): pl.pallas_call(kernel, out_shape=(pltpu.VMEM((TOKENS, WIDE), BF16), pltpu...]
where the time goes in v4:
time: 80.9 us; the launch traced here: 80.8 us
  Pallas kernels  80.2 us (99%)
    pallas_call x1, Pallas kernels, body(): pl.pallas_call(kernel, out_shape=(pltpu.VMEM((TOKENS, WIDE), BF16), pltpu...  77.6 us
    pallas_call x1, Pallas kernels, body(): pl.pallas_call(put_out, out_shape=(jax.ShapeDtypeStruct((TOKENS, WIDE), B...  2.62 us

profile of v4, /device:TPU:1, one launch (start us, length us, event | category | flops | bytes accessed | tf_op | source)
XLA Modules:
  0.0 80.8 jit_solution(2639562422544749805)
XLA Ops:
  0.6 77.6 %shard_map.76 = (bf16[1024,1184]{1,0:T(8,128)(2,1)S(1)}, f32[448,1184]{1,0:T(8,128)S(1)}, bf16[448,1184]{1,0:T(8,128)(2,1)S(1)}, bf16[8,448,1184]{2,1,0:T(8,128)...) custom-call(bf16[1024,224]{1,0:T(8,128)(2,1)} %bitcast.2, bf16[448,1184]{1,0:T(8,128)(2,1)} %weight.1, ...), custom_call_target="tpu_custom_call" | custom-call | tf_op jit(solution)/shard_map/pallas_call | solution.py:534
  78.2 2.6 %shard_map.77 = (bf16[1024,1184]{1,0:T(8,128)(2,1)}, f32[448,1184]{1,0:T(8,128)}, bf16[448,1184]{1,0:T(8,128)(2,1)}) custom-call(bf16[1024,1184]{1,0:T(8,128)(2,1)S(1)} %get-tuple-element.12.out_v, f32[448,1184]{1,0:T(8,128)S(1)} %get-tuple-element.13.step_v, bf16[448,1184]{1,0:T(8,128)(2,1)S(1)} %get-tuple-element.14.new_v, ...), custom_call_target="tpu_custom_call" | custom-call | tf_op jit(solution)/shard_map/pallas_call | solution.py:578

commit v5 on v4

--- a/solution.py
+++ b/solution.py
@@ -55,6 +55,7 @@
     bsem,
     tsem,
     asem,
+    esem,
     xsem,
     rsem,
     ssem,
@@ -116,6 +117,10 @@
             device_id_type=MESH,
         ).wait_recv()
 
+    barrier = pltpu.get_barrier_semaphore()
+    peers = [device for _, device in pop_peers + col_peers] + [far]
+    for device in peers:
+        pl.semaphore_signal(barrier, inc=1, device_id=device, device_id_type=MESH)
     own_noise = pltpu.make_async_copy(noise_in, noise_raw, lsem.at[0])
     own_out = pltpu.make_async_copy(out_in, out_raw, lsem.at[1])
     own_weight = pltpu.make_async_copy(weight, wbuf.at[0], lsem.at[2])
@@ -124,10 +129,6 @@
     for copy in (own_ranks, own_out, own_noise, own_weight, own_acts):
         copy.start()
 
-    barrier = pltpu.get_barrier_semaphore()
-    peers = [device for _, device in pop_peers + col_peers] + [far]
-    for device in peers:
-        pl.semaphore_signal(barrier, inc=1, device_id=device, device_id_type=MESH)
     pl.semaphore_wait(barrier, len(peers))
 
     def piece(h, j):
@@ -255,6 +256,9 @@
             preferred_element_type=F32,
         )
 
+    def half(slot, h, k):
+        return wbuf.at[slot, pl.ds(h * FEAT + k * 112, 112), pl.ds(*GROUPS[-1])]
+
     def relay(first, last):
         for j in range(first, last):
             w_arrive(3, 0, j)
@@ -272,8 +276,14 @@
         for i in range(first, last):
             h, j = to_pair[i]
             w_arrive(4, h, j)
-            w_send(4, h, j, 7, right)
-            w_send(4, h, j, 5, left)
+            if j < NG - 1 or h == 0:
+                w_send(4, h, j, 7, right)
+            else:
+                send(half(4, 1, 0), half(7, 1, 0), esem.at[1], right)
+            if j < NG - 1 or h == 1:
+                w_send(4, h, j, 5, left)
+            else:
+                send(half(4, 0, 0), half(5, 0, 0), esem.at[0], left)
 
     b_arrive(3, 0)
     b_send(3, 0, 2, right)
@@ -353,7 +363,7 @@
         )
         delta[pl.ds(h * FEAT, FEAT), :] = block
         squares += jnp.sum(block * block)
-    part[0] = jnp.full((8, 128), squares, F32)
+    part[0] = jnp.full((1, 128), squares, F32)
 
     for i, device in pop_peers:
         send(part.at[0], parts.at[8 + i], rsem.at[8 + i], device)
@@ -453,6 +463,8 @@
     for j in range(NG):
         w_arrive(3, 1, j)
         w_arrive(1, 0, j)
+    send(half(1, 0, 1), half(5, 0, 1), esem.at[2], pair)
+    send(half(3, 1, 1), half(7, 1, 1), esem.at[3], pair)
     blocks(1)
     pass_on(7, 9)
     blocks(3)
@@ -471,8 +483,11 @@
     for j in range(NG):
         for h in range(2):
             for slot in (5, 7, 6):
-                w_arrive(slot, h, j)
+                if j < NG - 1 or (slot, h) not in ((5, 0), (7, 1)):
+                    w_arrive(slot, h, j)
         if j == NG - 1:
+            for i, (slot, h, k) in enumerate(((5, 0, 0), (7, 1, 0), (5, 0, 1), (7, 1, 1))):
+                arrive(half(slot, h, k), esem.at[i])
             break
         cols = pl.ds(*GROUPS[j])
 
@@ -554,12 +569,13 @@
             pltpu.VMEM((PART, WIDE), BF16),
             pltpu.VMEM((TOKENS, PART), F32),
             pltpu.VMEM((ROWS, WIDE), F32),
-            pltpu.VMEM((3, 8, 128), F32),
-            pltpu.VMEM((16, 8, 128), F32),
+            pltpu.VMEM((3, 1, 128), F32),
+            pltpu.VMEM((16, 1, 128), F32),
             pltpu.SemaphoreType.DMA((POP * 2 * NG,)),
             pltpu.SemaphoreType.DMA((POP * 2,)),
             pltpu.SemaphoreType.DMA((POP * 2,)),
             pltpu.SemaphoreType.DMA((8,)),
+            pltpu.SemaphoreType.DMA((4,)),
             pltpu.SemaphoreType.DMA((19,)),
             pltpu.SemaphoreType.DMA((16,)),
             pltpu.SemaphoreType.DMA((192,)),

time: 80.9 us -> 80.6 us (level)
  no operation moved by 1% of the time
where the time goes in v5:
time: 80.6 us; the launch traced here: 80.5 us
  Pallas kernels  79.9 us (99%)
    pallas_call x1, Pallas kernels, body(): pl.pallas_call(kernel, out_shape=(pltpu.VMEM((TOKENS, WIDE), BF16), pltpu...  77.3 us
    pallas_call x1, Pallas kernels, body(): pl.pallas_call(put_out, out_shape=(jax.ShapeDtypeStruct((TOKENS, WIDE), B...  2.62 us

profile of v5, /device:TPU:1, one launch (start us, length us, event | category | flops | bytes accessed | tf_op | source)
XLA Modules:
  0.0 80.5 jit_solution(4285733528962035273)
XLA Ops:
  0.6 77.3 %shard_map.76 = (bf16[1024,1184]{1,0:T(8,128)(2,1)S(1)}, f32[448,1184]{1,0:T(8,128)S(1)}, bf16[448,1184]{1,0:T(8,128)(2,1)S(1)}, bf16[8,448,1184]{2,1,0:T(8,128)...) custom-call(bf16[1024,224]{1,0:T(8,128)(2,1)} %bitcast.2, bf16[448,1184]{1,0:T(8,128)(2,1)} %weight.1, ...), custom_call_target="tpu_custom_call" | custom-call | tf_op jit(solution)/shard_map/pallas_call | solution.py:549
  77.9 2.6 %shard_map.77 = (bf16[1024,1184]{1,0:T(8,128)(2,1)}, f32[448,1184]{1,0:T(8,128)}, bf16[448,1184]{1,0:T(8,128)(2,1)}) custom-call(bf16[1024,1184]{1,0:T(8,128)(2,1)S(1)} %get-tuple-element.12.out_v, f32[448,1184]{1,0:T(8,128)S(1)} %get-tuple-element.13.step_v, bf16[448,1184]{1,0:T(8,128)(2,1)S(1)} %get-tuple-element.14.new_v, ...), custom_call_target="tpu_custom_call" | custom-call | tf_op jit(solution)/shard_map/pallas_call | solution.py:594

commit v6 on v5

--- a/solution.py
+++ b/solution.py
@@ -390,6 +390,7 @@
     add_low(f_up)
     send(part.at[1], parts.at[8], rsem.at[8], far)
     own_to_pair(8, 10)
+    early = len(sent)
     across(0, 1)
     pass_on(0, 4)
 
@@ -480,6 +481,9 @@
     step = delta[...] * scale
     step_out[...] = step
     new_out[...] = (wbuf[0].astype(F32) + 0.01 * step).astype(BF16)
+    for copy in sent[:early]:
+        copy.wait_send()
+
     for j in range(NG):
         for h in range(2):
             for slot in (5, 7, 6):
@@ -500,7 +504,7 @@
             out[rows(i), cols] = value.astype(BF16)
 
 
-    for copy in sent:
+    for copy in sent[early:]:
         copy.wait_send()
 
 

time: 80.6 us -> 80.6 us (level)
  no operation moved by 1% of the time
where the time goes in v6:
time: 80.6 us; the launch traced here: 80.5 us
  Pallas kernels  79.9 us (99%)
    pallas_call x1, Pallas kernels, body(): pl.pallas_call(kernel, out_shape=(pltpu.VMEM((TOKENS, WIDE), BF16), pltpu...  77.3 us
    pallas_call x1, Pallas kernels, body(): pl.pallas_call(put_out, out_shape=(jax.ShapeDtypeStruct((TOKENS, WIDE), B...  2.62 us

profile of v6, /device:TPU:1, one launch (start us, length us, event | category | flops | bytes accessed | tf_op | source)
XLA Modules:
  0.0 80.5 jit_solution(18232811946865927846)
XLA Ops:
  0.6 77.3 %shard_map.76 = (bf16[1024,1184]{1,0:T(8,128)(2,1)S(1)}, f32[448,1184]{1,0:T(8,128)S(1)}, bf16[448,1184]{1,0:T(8,128)(2,1)S(1)}, bf16[8,448,1184]{2,1,0:T(8,128)...) custom-call(bf16[1024,224]{1,0:T(8,128)(2,1)} %bitcast.2, bf16[448,1184]{1,0:T(8,128)(2,1)} %weight.1, ...), custom_call_target="tpu_custom_call" | custom-call | tf_op jit(solution)/shard_map/pallas_call | solution.py:553
  77.9 2.6 %shard_map.77 = (bf16[1024,1184]{1,0:T(8,128)(2,1)}, f32[448,1184]{1,0:T(8,128)}, bf16[448,1184]{1,0:T(8,128)(2,1)}) custom-call(bf16[1024,1184]{1,0:T(8,128)(2,1)S(1)} %get-tuple-element.12.out_v, f32[448,1184]{1,0:T(8,128)S(1)} %get-tuple-element.13.step_v, bf16[448,1184]{1,0:T(8,128)(2,1)S(1)} %get-tuple-element.14.new_v, ...), custom_call_target="tpu_custom_call" | custom-call | tf_op jit(solution)/shard_map/pallas_call | solution.py:598
